TPU v7x, 32 devices: a whole 2x2x4 slice. The times are simulated.
32 devices in a mesh: seq: 16 (over z, y, core), head: 2 (over x).
Axes of the slice: x: 2, y: 2, z: 4, core: 2. Of those that a mesh axis runs over, the one named last changes fastest.
Arguments:
- tokens: bfloat16 [8192, 2048], P('seq', 'head'), may hold values from -200 to 200
- norm_gain: float32 [2, 2048], replicated, may hold values from 0.25 to 1.75
- w_query: bfloat16 [2, 2048, 2048], P(None, None, 'head'), may hold values from -0.35 to 0.35
- key_projection_weight: bfloat16 [2, 2048, 512], P(None, None, 'head'), may hold values from -0.35 to 0.35
- value_projection_weight: bfloat16 [2, 2048, 512], P(None, None, 'head'), may hold values from -0.125 to 0.125
- w_out: bfloat16 [2, 2048, 2048], P(None, 'head'), may hold values from -0.125 to 0.125
- counts: int32 [16], replicated, may hold values from 128 to 512
Outputs:
- hidden_out: bfloat16 [8192, 2048], P('seq', 'head')
Inputs may be any that keep to these rules, and one draw needn't show every extreme that they name: The first counts[b] tokens of block b of 512 positions are valid keys; the rest of the block is padding that no query uses as a key.
All inputs are finite; a program needn't handle non-finite values.
Results may differ from a plain program's by a relative error of at most 0.02.
The roundings to bfloat16 on the way count: a program that leaves them out, or rounds other values in their place, can miss the bound.
Values may be sent and summed in bfloat16 or wider, within the bound.
A program may use at most 128 MiB of HBM per device.

v0:
```python
import math
import jax
import jax.numpy as jnp
from jax import lax
from jax.sharding import PartitionSpec as P

MODEL_WIDTH = 2048
HEAD_SIZE = 128
WINDOW = 4096
LAYER_COUNT = 2
norm_epsilon = 1e-05
rope_base = 10000.0


def passed_along(value, axis, steps):
    count = lax.axis_size(axis)
    initial, last = (max(0, -steps), min(count, count - steps))
    return lax.ppermute(value, axis, [(source, source + steps) for source in range(initial, last)])


def rotate_heads(projected, token_positions, head_count):
    row_total = projected.shape[0]
    shaped = projected.reshape(row_total, head_count, HEAD_SIZE)
    half_dim = HEAD_SIZE // 2
    inverse = jnp.power(
        jnp.float32(rope_base), -2.0 * jnp.arange(half_dim, dtype=jnp.float32) / HEAD_SIZE
    )
    angles = token_positions.astype(jnp.float32)[:, None] * inverse[None, :]
    cosine_table = jnp.cos(angles)[:, None, :]
    sine_table = jnp.sin(angles)[:, None, :]
    first_half = shaped[..., :half_dim]
    second_half = shaped[..., half_dim:]
    rotated = jnp.concatenate(
        [
            first_half * cosine_table - second_half * sine_table,
            second_half * cosine_table + first_half * sine_table,
        ],
        axis=-1,
    )
    return rotated.astype(jnp.bfloat16)


def block_mask(counts, block_index, rows_here, span_blocks):
    key_length = (span_blocks + 1) * rows_here
    first_row = block_index * rows_here
    query_positions = first_row + jnp.arange(rows_here, dtype=jnp.int32)
    key_positions = first_row - span_blocks * rows_here + jnp.arange(key_length, dtype=jnp.int32)
    block_numbers = block_index - span_blocks + jnp.arange(span_blocks + 1, dtype=jnp.int32)
    table_size = counts.shape[0]
    matches = block_numbers[:, None] == jnp.arange(table_size, dtype=jnp.int32)[None, :]
    block_counts = jnp.sum(jnp.where(matches, counts[None, :], 0), axis=1)
    within_block = jnp.arange(rows_here, dtype=jnp.int32)
    valid_keys = (
        (block_numbers[:, None] >= 0) & (within_block[None, :] < block_counts[:, None])
    ).reshape(key_length)
    allowed = valid_keys[None, :] & (key_positions[None, :] <= query_positions[:, None])
    return allowed & (query_positions[:, None] - key_positions[None, :] < WINDOW)


def attend_local(queries, stacked, allowed):
    rows_here = queries.shape[0]
    local_heads = queries.shape[1]
    block_total = stacked.shape[0]
    local_groups = stacked.shape[3] // HEAD_SIZE
    key_length = block_total * rows_here
    key_heads = stacked[:, 0].reshape(key_length, local_groups, HEAD_SIZE).transpose(1, 0, 2)
    value_heads = stacked[:, 1].reshape(key_length, local_groups, HEAD_SIZE).transpose(1, 0, 2)
    query_heads = queries.transpose(1, 0, 2)
    group_length = local_heads // local_groups
    scale_factor = 1.0 / math.sqrt(HEAD_SIZE)

    def one_head(head_number):
        query_one = lax.dynamic_index_in_dim(query_heads, head_number, 0, keepdims=False)
        key_one = lax.dynamic_index_in_dim(
            key_heads, head_number // group_length, 0, keepdims=False
        )
        value_one = lax.dynamic_index_in_dim(
            value_heads, head_number // group_length, 0, keepdims=False
        )
        scores = (
            lax.dot_general(
                query_one, key_one, (((1,), (1,)), ((), ())), preferred_element_type=jnp.float32
            )
            * scale_factor
        )
        scores = jnp.where(allowed, scores, -jnp.inf)
        largest = jnp.max(scores, axis=1, keepdims=True)
        weights = jnp.exp(scores - largest)
        weights = (weights / jnp.sum(weights, axis=1, keepdims=True)).astype(jnp.bfloat16)
        return jnp.dot(weights, value_one, preferred_element_type=jnp.float32).astype(jnp.bfloat16)

    blended = lax.map(one_head, jnp.arange(local_heads, dtype=jnp.int32))
    return blended.transpose(1, 0, 2).reshape(rows_here, local_heads * HEAD_SIZE)


def relay_blocks(stacked_own, span_blocks):
    zero_blocks = jnp.zeros((span_blocks,) + stacked_own.shape, stacked_own.dtype)

    def step_once(step_number, carried):
        passing, collected = carried
        passing = passed_along(passing, "seq", 1)
        collected = lax.dynamic_update_index_in_dim(
            collected, passing, span_blocks - 1 - step_number, 0
        )
        return (passing, collected)

    passing, collected = lax.fori_loop(0, span_blocks, step_once, (stacked_own, zero_blocks))
    return jnp.concatenate([collected, stacked_own[None]], axis=0)


def per_device(
    tokens, norm_gain, w_query, key_projection_weight, value_projection_weight, w_out, counts
):
    rows_here = tokens.shape[0]
    half_width = tokens.shape[1]
    span_blocks = WINDOW // rows_here
    block_index = lax.axis_index("seq")
    head_index = lax.axis_index("head")
    token_positions = block_index * rows_here + jnp.arange(rows_here, dtype=jnp.int32)
    allowed = block_mask(counts, block_index, rows_here, span_blocks)
    local_query = w_query.shape[2] // HEAD_SIZE
    local_kv = key_projection_weight.shape[2] // HEAD_SIZE
    hidden = tokens
    for layer_position in range(LAYER_COUNT):
        gain_row = norm_gain[layer_position]
        query_weight = w_query[layer_position]
        key_weight = key_projection_weight[layer_position]
        value_weight = value_projection_weight[layer_position]
        widened = hidden.astype(jnp.float32)
        total_squares = lax.psum(jnp.sum(widened * widened, axis=1), "head")
        gain_part = lax.dynamic_slice_in_dim(gain_row, head_index * half_width, half_width, 0)
        normed_part = (
            widened
            * lax.rsqrt(total_squares / MODEL_WIDTH + norm_epsilon)[:, None]
            * gain_part[None, :]
        ).astype(jnp.bfloat16)

        def project_piece(
            running, piece_rows, offset, weights_now=(query_weight, key_weight, value_weight)
        ):
            width_here = piece_rows.shape[1]
            return tuple(
                (
                    jnp.dot(piece_rows, weight, preferred_element_type=jnp.float32)
                    for weight in weights_now
                )
            )

        starting = (
            jnp.zeros((rows_here, query_weight.shape[1]), jnp.float32),
            jnp.zeros((rows_here, key_weight.shape[1]), jnp.float32),
            jnp.zeros((rows_here, value_weight.shape[1]), jnp.float32),
        )
        query_raw, key_raw, value_raw = project_piece(
            starting, lax.all_gather(normed_part, "head", axis=1, tiled=True), jnp.int32(0)
        )
        queries = rotate_heads(query_raw, token_positions, local_query)
        keys_own = rotate_heads(key_raw, token_positions, local_kv).reshape(
            rows_here, local_kv * HEAD_SIZE
        )
        values_own = value_raw.astype(jnp.bfloat16)
        stacked_own = jnp.stack([keys_own, values_own])
        stacked = relay_blocks(stacked_own, span_blocks)
        attended = attend_local(queries, stacked, allowed)
        partial_product = jnp.dot(
            attended, w_out[layer_position], preferred_element_type=jnp.float32
        )
        rounded = lax.optimization_barrier(partial_product.astype(jnp.bfloat16)).astype(jnp.float32)
        own_share = lax.psum_scatter(
            rounded.astype(jnp.bfloat16), "head", scatter_dimension=1, tiled=True
        ).astype(jnp.float32)
        hidden = (hidden.astype(jnp.float32) + own_share).astype(jnp.bfloat16)
    return hidden


def solution(mesh):
    return jax.shard_map(
        per_device,
        mesh=mesh,
        in_specs=(
            P("seq", "head"),
            P(),
            P(None, None, "head"),
            P(None, None, "head"),
            P(None, None, "head"),
            P(None, "head", None),
            P(),
        ),
        out_specs=P("seq", "head"),
        check_vma=False,
    )
```

profile of v0, /device:TPU:0, one launch (start us, length us, event | category | flops | bytes accessed | tf_op | source)
XLA Modules:
  0.0 653.0 jit_solution(17317574865191985672)
XLA Ops:
  25.7 6.7 %copy.30 = bf16[1024,2048]{1,0:T(8,128)(2,1)} copy(bf16[1024,2048]{0,1:T(8,128)(2,1)} %get-tuple-element.469) | data formatting | bytes 8388608 | tf_op jit(solution)/shard_map/dot_general | solution.py:144
  34.5 17.8 %all-gather.3.cloned.1.call-done = bf16[512,2048]{1,0:T(8,128)(2,1)} async-done(((bf16[512,1024]{1,0:T(8,128)(2,1)}), bf16[512,2048]{1,0:T(8,128)(2,1)}) %all-gather.3.cloned.1.call-update) | async-done | bytes 2097168 | tf_op jit(solution)/shard_map/all_gather | solution.py:155
  59.9 83.0 %while.56 = (s32[]{:T(128)}, bf16[2,512,256]{2,1,0:T(8,128)(2,1)S(1)}, bf16[8,2,512,256]{3,2,1,0:T(8,128)(2,1)}, s32[]{:T(128)}, s32[]{:T(128)}, /*index=5*/s32[]{:T(128)}, s32[]{:T(128)}) while((s32[]{:T(128)}, bf16[2,512,256]{2,1,0:T(8,128)(2,1)S(1)}, bf16[8,2,512,256]{3,2,1,0:T(8,128)(2,1)}, s32[]{:T(128)}, s32[]{:T(128)}, ...), condition=%wide.region_3.4_spmd, body=%wide.region_2.3_spmd.sunk | while | flops 6 | bytes 4194471 | solution.py:107
  63.9 8.4 %collective-permute-start = (bf16[2,512,256]{2,1,0:T(8,128)(2,1)S(1)}, bf16[2,512,256]{2,1,0:T(8,128)(2,1)S(1)}, u32[]{:S(2)}, u32[]{:S(2)}) collective-permute-start(bf16[2,512,256]{2,1,0:T(8,128)(2,1)S(1)} %get-tuple-element.659), channel_id=1, source_target_pairs={{0,2},{2,4},{4,6},{6,8},{8,10},{10,12},{12,14},{14,16},{16,18},{18... | collective-permute-start | bytes 1572872 | tf_op jit(solution)/shard_map/while/body/eval_jaxpr/ppermute | solution.py:18
  74.7 9.0 %collective-permute-start = (bf16[2,512,256]{2,1,0:T(8,128)(2,1)S(1)}, bf16[2,512,256]{2,1,0:T(8,128)(2,1)S(1)}, u32[]{:S(2)}, u32[]{:S(2)}) collective-permute-start(bf16[2,512,256]{2,1,0:T(8,128)(2,1)S(1)} %get-tuple-element.659), channel_id=1, source_target_pairs={{0,2},{2,4},{4,6},{6,8},{8,10},{10,12},{12,14},{14,16},{16,18},{18... | collective-permute-start | bytes 1572872 | tf_op jit(solution)/shard_map/while/body/eval_jaxpr/ppermute | solution.py:18
  86.1 9.0 %collective-permute-start = (bf16[2,512,256]{2,1,0:T(8,128)(2,1)S(1)}, bf16[2,512,256]{2,1,0:T(8,128)(2,1)S(1)}, u32[]{:S(2)}, u32[]{:S(2)}) collective-permute-start(bf16[2,512,256]{2,1,0:T(8,128)(2,1)S(1)} %get-tuple-element.659), channel_id=1, source_target_pairs={{0,2},{2,4},{4,6},{6,8},{8,10},{10,12},{12,14},{14,16},{16,18},{18... | collective-permute-start | bytes 1572872 | tf_op jit(solution)/shard_map/while/body/eval_jaxpr/ppermute | solution.py:18
  97.4 9.0 %collective-permute-start = (bf16[2,512,256]{2,1,0:T(8,128)(2,1)S(1)}, bf16[2,512,256]{2,1,0:T(8,128)(2,1)S(1)}, u32[]{:S(2)}, u32[]{:S(2)}) collective-permute-start(bf16[2,512,256]{2,1,0:T(8,128)(2,1)S(1)} %get-tuple-element.659), channel_id=1, source_target_pairs={{0,2},{2,4},{4,6},{6,8},{8,10},{10,12},{12,14},{14,16},{16,18},{18... | collective-permute-start | bytes 1572872 | tf_op jit(solution)/shard_map/while/body/eval_jaxpr/ppermute | solution.py:18
  108.8 9.0 %collective-permute-start = (bf16[2,512,256]{2,1,0:T(8,128)(2,1)S(1)}, bf16[2,512,256]{2,1,0:T(8,128)(2,1)S(1)}, u32[]{:S(2)}, u32[]{:S(2)}) collective-permute-start(bf16[2,512,256]{2,1,0:T(8,128)(2,1)S(1)} %get-tuple-element.659), channel_id=1, source_target_pairs={{0,2},{2,4},{4,6},{6,8},{8,10},{10,12},{12,14},{14,16},{16,18},{18... | collective-permute-start | bytes 1572872 | tf_op jit(solution)/shard_map/while/body/eval_jaxpr/ppermute | solution.py:18
  120.2 9.0 %collective-permute-start = (bf16[2,512,256]{2,1,0:T(8,128)(2,1)S(1)}, bf16[2,512,256]{2,1,0:T(8,128)(2,1)S(1)}, u32[]{:S(2)}, u32[]{:S(2)}) collective-permute-start(bf16[2,512,256]{2,1,0:T(8,128)(2,1)S(1)} %get-tuple-element.659), channel_id=1, source_target_pairs={{0,2},{2,4},{4,6},{6,8},{8,10},{10,12},{12,14},{14,16},{16,18},{18... | collective-permute-start | bytes 1572872 | tf_op jit(solution)/shard_map/while/body/eval_jaxpr/ppermute | solution.py:18
  131.6 9.0 %collective-permute-start = (bf16[2,512,256]{2,1,0:T(8,128)(2,1)S(1)}, bf16[2,512,256]{2,1,0:T(8,128)(2,1)S(1)}, u32[]{:S(2)}, u32[]{:S(2)}) collective-permute-start(bf16[2,512,256]{2,1,0:T(8,128)(2,1)S(1)} %get-tuple-element.659), channel_id=1, source_target_pairs={{0,2},{2,4},{4,6},{6,8},{8,10},{10,12},{12,14},{14,16},{16,18},{18... | collective-permute-start | bytes 1572872 | tf_op jit(solution)/shard_map/while/body/eval_jaxpr/ppermute | solution.py:18
  166.5 109.6 %while.58 = (s32[]{:T(128)}, bf16[8,512,128]{1,2,0:T(8,128)(2,1)}, s32[8]{0:T(128)S(1)}, bf16[8,512,128]{1,2,0:T(8,128)(2,1)S(1)}, bf16[2,4608,128]{2,1,0:T(8,12...) while((s32[]{:T(128)}, bf16[8,512,128]{1,2,0:T(8,128)(2,1)}, ...), condition=%wide.region_8.9_spmd.clone, body=%wide.region_5.8_spmd.clone.sunk | while | flops 1238694912 | bytes 40933264 | solution.py:92
  282.4 46.2 %reduce-scatter.3.cloned.1.call-done = bf16[512,1024]{1,0:T(8,128)(2,1)} async-done(((bf16[512,2048]{1,0:T(8,128)(2,1)}), bf16[512,1024]{1,0:T(8,128)(2,1)}) %reduce-scatter.3.cloned.1.call-update) | async-done | bytes 1048592 | tf_op jit(solution)/shard_map/reduce_scatter | solution.py:169
  337.6 6.6 %copy.37 = bf16[1024,2048]{1,0:T(8,128)(2,1)} copy(bf16[1024,2048]{0,1:T(8,128)(2,1)} %get-tuple-element.470) | data formatting | bytes 8388608 | tf_op jit(solution)/shard_map/dot_general | solution.py:144
  344.2 25.8 %all-gather.5.cloned.1.call-done = bf16[512,2048]{1,0:T(8,128)(2,1)} async-done(((bf16[512,1024]{1,0:T(8,128)(2,1)}), bf16[512,2048]{1,0:T(8,128)(2,1)}) %all-gather.5.cloned.1.call-update) | async-done | bytes 2097168 | tf_op jit(solution)/shard_map/all_gather | solution.py:155
  377.6 83.0 %while.57 = (s32[]{:T(128)}, bf16[2,512,256]{2,1,0:T(8,128)(2,1)S(1)}, bf16[8,2,512,256]{3,2,1,0:T(8,128)(2,1)}, s32[]{:T(128)}, s32[]{:T(128)}, /*index=5*/s32[]{:T(128)}, s32[]{:T(128)}) while((s32[]{:T(128)}, bf16[2,512,256]{2,1,0:T(8,128)(2,1)S(1)}, bf16[8,2,512,256]{3,2,1,0:T(8,128)(2,1)}, s32[]{:T(128)}, s32[]{:T(128)}, ...), condition=%wide.region_13.14_spmd, body=%wide.region_12.13_spmd.sunk | while | flops 6 | bytes 4194471 | solution.py:107
  381.6 8.4 %collective-permute-start.1 = (bf16[2,512,256]{2,1,0:T(8,128)(2,1)S(1)}, bf16[2,512,256]{2,1,0:T(8,128)(2,1)S(1)}, u32[]{:S(2)}, u32[]{:S(2)}) collective-permute-start(bf16[2,512,256]{2,1,0:T(8,128)(2,1)S(1)} %get-tuple-element.725), channel_id=1, source_target_pairs={{0,2},{2,4},{4,6},{6,8},{8,10},{10,12},{12,14},{14,16},{16,18},{18... | collective-permute-start | bytes 1572872 | tf_op jit(solution)/shard_map/while/body/eval_jaxpr/ppermute | solution.py:18
  392.4 9.0 %collective-permute-start.1 = (bf16[2,512,256]{2,1,0:T(8,128)(2,1)S(1)}, bf16[2,512,256]{2,1,0:T(8,128)(2,1)S(1)}, u32[]{:S(2)}, u32[]{:S(2)}) collective-permute-start(bf16[2,512,256]{2,1,0:T(8,128)(2,1)S(1)} %get-tuple-element.725), channel_id=1, source_target_pairs={{0,2},{2,4},{4,6},{6,8},{8,10},{10,12},{12,14},{14,16},{16,18},{18... | collective-permute-start | bytes 1572872 | tf_op jit(solution)/shard_map/while/body/eval_jaxpr/ppermute | solution.py:18
  403.7 9.0 %collective-permute-start.1 = (bf16[2,512,256]{2,1,0:T(8,128)(2,1)S(1)}, bf16[2,512,256]{2,1,0:T(8,128)(2,1)S(1)}, u32[]{:S(2)}, u32[]{:S(2)}) collective-permute-start(bf16[2,512,256]{2,1,0:T(8,128)(2,1)S(1)} %get-tuple-element.725), channel_id=1, source_target_pairs={{0,2},{2,4},{4,6},{6,8},{8,10},{10,12},{12,14},{14,16},{16,18},{18... | collective-permute-start | bytes 1572872 | tf_op jit(solution)/shard_map/while/body/eval_jaxpr/ppermute | solution.py:18
  415.1 9.0 %collective-permute-start.1 = (bf16[2,512,256]{2,1,0:T(8,128)(2,1)S(1)}, bf16[2,512,256]{2,1,0:T(8,128)(2,1)S(1)}, u32[]{:S(2)}, u32[]{:S(2)}) collective-permute-start(bf16[2,512,256]{2,1,0:T(8,128)(2,1)S(1)} %get-tuple-element.725), channel_id=1, source_target_pairs={{0,2},{2,4},{4,6},{6,8},{8,10},{10,12},{12,14},{14,16},{16,18},{18... | collective-permute-start | bytes 1572872 | tf_op jit(solution)/shard_map/while/body/eval_jaxpr/ppermute | solution.py:18
  426.5 9.0 %collective-permute-start.1 = (bf16[2,512,256]{2,1,0:T(8,128)(2,1)S(1)}, bf16[2,512,256]{2,1,0:T(8,128)(2,1)S(1)}, u32[]{:S(2)}, u32[]{:S(2)}) collective-permute-start(bf16[2,512,256]{2,1,0:T(8,128)(2,1)S(1)} %get-tuple-element.725), channel_id=1, source_target_pairs={{0,2},{2,4},{4,6},{6,8},{8,10},{10,12},{12,14},{14,16},{16,18},{18... | collective-permute-start | bytes 1572872 | tf_op jit(solution)/shard_map/while/body/eval_jaxpr/ppermute | solution.py:18
  437.9 9.0 %collective-permute-start.1 = (bf16[2,512,256]{2,1,0:T(8,128)(2,1)S(1)}, bf16[2,512,256]{2,1,0:T(8,128)(2,1)S(1)}, u32[]{:S(2)}, u32[]{:S(2)}) collective-permute-start(bf16[2,512,256]{2,1,0:T(8,128)(2,1)S(1)} %get-tuple-element.725), channel_id=1, source_target_pairs={{0,2},{2,4},{4,6},{6,8},{8,10},{10,12},{12,14},{14,16},{16,18},{18... | collective-permute-start | bytes 1572872 | tf_op jit(solution)/shard_map/while/body/eval_jaxpr/ppermute | solution.py:18
  449.3 9.0 %collective-permute-start.1 = (bf16[2,512,256]{2,1,0:T(8,128)(2,1)S(1)}, bf16[2,512,256]{2,1,0:T(8,128)(2,1)S(1)}, u32[]{:S(2)}, u32[]{:S(2)}) collective-permute-start(bf16[2,512,256]{2,1,0:T(8,128)(2,1)S(1)} %get-tuple-element.725), channel_id=1, source_target_pairs={{0,2},{2,4},{4,6},{6,8},{8,10},{10,12},{12,14},{14,16},{16,18},{18... | collective-permute-start | bytes 1572872 | tf_op jit(solution)/shard_map/while/body/eval_jaxpr/ppermute | solution.py:18
  483.7 107.6 %while.59 = (s32[]{:T(128)}, bf16[8,512,128]{1,2,0:T(8,128)(2,1)S(1)}, s32[8]{0:T(128)S(1)}, bf16[8,512,128]{1,2,0:T(8,128)(2,1)S(1)}, bf16[2,4608,128]{2,1,0:T(...) while((s32[]{:T(128)}, ...), condition=%wide.region_17.18_spmd.clone, body=%wide.region_14.17_spmd.clone.sunk | while | flops 1238694912 | bytes 40932756 | solution.py:92
  597.2 46.3 %reduce-scatter.5.cloned.1.call-done = bf16[512,1024]{1,0:T(8,128)(2,1)} async-done(((bf16[512,2048]{1,0:T(8,128)(2,1)}), bf16[512,1024]{1,0:T(8,128)(2,1)}) %reduce-scatter.5.cloned.1.call-update) | async-done | bytes 1048592 | tf_op jit(solution)/shard_map/reduce_scatter | solution.py:169
  (273 shorter events, 304.7 us)
Async XLA Ops:
  6.5 45.8 %all-gather.3.cloned.1.call-start = ((), (), s32[]{:S(2)}) async-start(), calls=%async_computation.2 | async-start | bytes 3145728 | tf_op jit(solution)/shard_map/all_gather | solution.py:155
  17.3 311.4 %reduce-scatter.3.cloned.1.call-start = ((), (), s32[]{:S(2)}) async-start(), calls=%async_computation.3 | async-start | bytes 3145728 | tf_op jit(solution)/shard_map/reduce_scatter | solution.py:169
  25.7 6.7 %copy-start.14 = (s32[16]{0:T(128)S(1)}, s32[16]{0:T(128)}, u32[]{:S(2)}) copy-start(s32[16]{0:T(128)} %param.21) | copy-start | bytes 196
  34.4 20.2 %copy-start.5 = (f32[512,64]{0,1:T(8,128)}, f32[512,64]{0,1:T(8,128)S(1)}, u32[]{:S(2)}) copy-start(f32[512,64]{0,1:T(8,128)S(1)} %get-tuple-element.492) | copy-start | bytes 393220
  59.9 3.1 collective-permute-start
  63.9 9.9 %collective-permute-start = (bf16[2,512,256]{2,1,0:T(8,128)(2,1)S(1)}, bf16[2,512,256]{2,1,0:T(8,128)(2,1)S(1)}, u32[]{:S(2)}, u32[]{:S(2)}) collective-permute-start(bf16[2,512,256]{2,1,0:T(8,128)(2,1)S(1)} %get-tuple-element.659), channel_id=1, source_target_pairs={{0,2},{2,4},{4,6},{6,8},{8,10},{10,12},{12,14},{14,16},{16,18},{18... | collective-permute-start | bytes 1572872 | tf_op jit(solution)/shard_map/while/body/eval_jaxpr/ppermute | solution.py:18
  74.7 10.5 %collective-permute-start = (bf16[2,512,256]{2,1,0:T(8,128)(2,1)S(1)}, bf16[2,512,256]{2,1,0:T(8,128)(2,1)S(1)}, u32[]{:S(2)}, u32[]{:S(2)}) collective-permute-start(bf16[2,512,256]{2,1,0:T(8,128)(2,1)S(1)} %get-tuple-element.659), channel_id=1, source_target_pairs={{0,2},{2,4},{4,6},{6,8},{8,10},{10,12},{12,14},{14,16},{16,18},{18... | collective-permute-start | bytes 1572872 | tf_op jit(solution)/shard_map/while/body/eval_jaxpr/ppermute | solution.py:18
  86.1 10.5 %collective-permute-start = (bf16[2,512,256]{2,1,0:T(8,128)(2,1)S(1)}, bf16[2,512,256]{2,1,0:T(8,128)(2,1)S(1)}, u32[]{:S(2)}, u32[]{:S(2)}) collective-permute-start(bf16[2,512,256]{2,1,0:T(8,128)(2,1)S(1)} %get-tuple-element.659), channel_id=1, source_target_pairs={{0,2},{2,4},{4,6},{6,8},{8,10},{10,12},{12,14},{14,16},{16,18},{18... | collective-permute-start | bytes 1572872 | tf_op jit(solution)/shard_map/while/body/eval_jaxpr/ppermute | solution.py:18
  97.4 10.5 %collective-permute-start = (bf16[2,512,256]{2,1,0:T(8,128)(2,1)S(1)}, bf16[2,512,256]{2,1,0:T(8,128)(2,1)S(1)}, u32[]{:S(2)}, u32[]{:S(2)}) collective-permute-start(bf16[2,512,256]{2,1,0:T(8,128)(2,1)S(1)} %get-tuple-element.659), channel_id=1, source_target_pairs={{0,2},{2,4},{4,6},{6,8},{8,10},{10,12},{12,14},{14,16},{16,18},{18... | collective-permute-start | bytes 1572872 | tf_op jit(solution)/shard_map/while/body/eval_jaxpr/ppermute | solution.py:18
  108.8 10.5 %collective-permute-start = (bf16[2,512,256]{2,1,0:T(8,128)(2,1)S(1)}, bf16[2,512,256]{2,1,0:T(8,128)(2,1)S(1)}, u32[]{:S(2)}, u32[]{:S(2)}) collective-permute-start(bf16[2,512,256]{2,1,0:T(8,128)(2,1)S(1)} %get-tuple-element.659), channel_id=1, source_target_pairs={{0,2},{2,4},{4,6},{6,8},{8,10},{10,12},{12,14},{14,16},{16,18},{18... | collective-permute-start | bytes 1572872 | tf_op jit(solution)/shard_map/while/body/eval_jaxpr/ppermute | solution.py:18
  120.2 10.5 %collective-permute-start = (bf16[2,512,256]{2,1,0:T(8,128)(2,1)S(1)}, bf16[2,512,256]{2,1,0:T(8,128)(2,1)S(1)}, u32[]{:S(2)}, u32[]{:S(2)}) collective-permute-start(bf16[2,512,256]{2,1,0:T(8,128)(2,1)S(1)} %get-tuple-element.659), channel_id=1, source_target_pairs={{0,2},{2,4},{4,6},{6,8},{8,10},{10,12},{12,14},{14,16},{16,18},{18... | collective-permute-start | bytes 1572872 | tf_op jit(solution)/shard_map/while/body/eval_jaxpr/ppermute | solution.py:18
  131.6 10.5 %collective-permute-start = (bf16[2,512,256]{2,1,0:T(8,128)(2,1)S(1)}, bf16[2,512,256]{2,1,0:T(8,128)(2,1)S(1)}, u32[]{:S(2)}, u32[]{:S(2)}) collective-permute-start(bf16[2,512,256]{2,1,0:T(8,128)(2,1)S(1)} %get-tuple-element.659), channel_id=1, source_target_pairs={{0,2},{2,4},{4,6},{6,8},{8,10},{10,12},{12,14},{14,16},{16,18},{18... | collective-permute-start | bytes 1572872 | tf_op jit(solution)/shard_map/while/body/eval_jaxpr/ppermute | solution.py:18
  282.3 46.3 %copy-start = (bf16[512,1024]{1,0:T(8,128)(2,1)S(1)}, bf16[512,1024]{1,0:T(8,128)(2,1)}, u32[]{:S(2)}) copy-start(bf16[512,1024]{1,0:T(8,128)(2,1)} %param.15) | copy-start | bytes 3145732
  282.4 87.6 %all-gather.5.cloned.1.call-start = ((), (), s32[]{:S(2)}) async-start(), calls=%async_computation.4 | async-start | bytes 3145728 | tf_op jit(solution)/shard_map/all_gather | solution.py:155
  336.7 306.7 %reduce-scatter.5.cloned.1.call-start = ((), (), s32[]{:S(2)}) async-start(), calls=%async_computation.5 | async-start | bytes 3145728 | tf_op jit(solution)/shard_map/reduce_scatter | solution.py:169
  377.6 3.1 collective-permute-start.1
  381.6 9.9 %collective-permute-start.1 = (bf16[2,512,256]{2,1,0:T(8,128)(2,1)S(1)}, bf16[2,512,256]{2,1,0:T(8,128)(2,1)S(1)}, u32[]{:S(2)}, u32[]{:S(2)}) collective-permute-start(bf16[2,512,256]{2,1,0:T(8,128)(2,1)S(1)} %get-tuple-element.725), channel_id=1, source_target_pairs={{0,2},{2,4},{4,6},{6,8},{8,10},{10,12},{12,14},{14,16},{16,18},{18... | collective-permute-start | bytes 1572872 | tf_op jit(solution)/shard_map/while/body/eval_jaxpr/ppermute | solution.py:18
  392.4 10.5 %collective-permute-start.1 = (bf16[2,512,256]{2,1,0:T(8,128)(2,1)S(1)}, bf16[2,512,256]{2,1,0:T(8,128)(2,1)S(1)}, u32[]{:S(2)}, u32[]{:S(2)}) collective-permute-start(bf16[2,512,256]{2,1,0:T(8,128)(2,1)S(1)} %get-tuple-element.725), channel_id=1, source_target_pairs={{0,2},{2,4},{4,6},{6,8},{8,10},{10,12},{12,14},{14,16},{16,18},{18... | collective-permute-start | bytes 1572872 | tf_op jit(solution)/shard_map/while/body/eval_jaxpr/ppermute | solution.py:18
  403.7 10.5 %collective-permute-start.1 = (bf16[2,512,256]{2,1,0:T(8,128)(2,1)S(1)}, bf16[2,512,256]{2,1,0:T(8,128)(2,1)S(1)}, u32[]{:S(2)}, u32[]{:S(2)}) collective-permute-start(bf16[2,512,256]{2,1,0:T(8,128)(2,1)S(1)} %get-tuple-element.725), channel_id=1, source_target_pairs={{0,2},{2,4},{4,6},{6,8},{8,10},{10,12},{12,14},{14,16},{16,18},{18... | collective-permute-start | bytes 1572872 | tf_op jit(solution)/shard_map/while/body/eval_jaxpr/ppermute | solution.py:18
  415.1 10.5 %collective-permute-start.1 = (bf16[2,512,256]{2,1,0:T(8,128)(2,1)S(1)}, bf16[2,512,256]{2,1,0:T(8,128)(2,1)S(1)}, u32[]{:S(2)}, u32[]{:S(2)}) collective-permute-start(bf16[2,512,256]{2,1,0:T(8,128)(2,1)S(1)} %get-tuple-element.725), channel_id=1, source_target_pairs={{0,2},{2,4},{4,6},{6,8},{8,10},{10,12},{12,14},{14,16},{16,18},{18... | collective-permute-start | bytes 1572872 | tf_op jit(solution)/shard_map/while/body/eval_jaxpr/ppermute | solution.py:18
  426.5 10.5 %collective-permute-start.1 = (bf16[2,512,256]{2,1,0:T(8,128)(2,1)S(1)}, bf16[2,512,256]{2,1,0:T(8,128)(2,1)S(1)}, u32[]{:S(2)}, u32[]{:S(2)}) collective-permute-start(bf16[2,512,256]{2,1,0:T(8,128)(2,1)S(1)} %get-tuple-element.725), channel_id=1, source_target_pairs={{0,2},{2,4},{4,6},{6,8},{8,10},{10,12},{12,14},{14,16},{16,18},{18... | collective-permute-start | bytes 1572872 | tf_op jit(solution)/shard_map/while/body/eval_jaxpr/ppermute | solution.py:18
  437.9 10.5 %collective-permute-start.1 = (bf16[2,512,256]{2,1,0:T(8,128)(2,1)S(1)}, bf16[2,512,256]{2,1,0:T(8,128)(2,1)S(1)}, u32[]{:S(2)}, u32[]{:S(2)}) collective-permute-start(bf16[2,512,256]{2,1,0:T(8,128)(2,1)S(1)} %get-tuple-element.725), channel_id=1, source_target_pairs={{0,2},{2,4},{4,6},{6,8},{8,10},{10,12},{12,14},{14,16},{16,18},{18... | collective-permute-start | bytes 1572872 | tf_op jit(solution)/shard_map/while/body/eval_jaxpr/ppermute | solution.py:18
  449.3 10.5 %collective-permute-start.1 = (bf16[2,512,256]{2,1,0:T(8,128)(2,1)S(1)}, bf16[2,512,256]{2,1,0:T(8,128)(2,1)S(1)}, u32[]{:S(2)}, u32[]{:S(2)}) collective-permute-start(bf16[2,512,256]{2,1,0:T(8,128)(2,1)S(1)} %get-tuple-element.725), channel_id=1, source_target_pairs={{0,2},{2,4},{4,6},{6,8},{8,10},{10,12},{12,14},{14,16},{16,18},{18... | collective-permute-start | bytes 1572872 | tf_op jit(solution)/shard_map/while/body/eval_jaxpr/ppermute | solution.py:18
  597.1 46.3 %copy-start.2 = (bf16[512,1024]{1,0:T(8,128)(2,1)S(1)}, bf16[512,1024]{1,0:T(8,128)(2,1)}, u32[]{:S(2)}) copy-start(bf16[512,1024]{1,0:T(8,128)(2,1)} %reduce-scatter.3.cloned.1.call-done) | copy-start | bytes 3145732
  (25 other events, 51.4 us)
Sparse Core Ops, SparseCore 0:
  17.4 34.8 all-gather.2
  282.5 46.1 reduce-scatter.2
  336.8 33.0 all-gather.4
  597.3 46.1 reduce-scatter.4
where the time goes:
time: 664 us; the launch traced here: 653 us
  waiting for transfers between devices  160 us (24%)
  matrix products  144 us (22%)
  starting transfers between devices  128 us (19%)
  local copies, waits for them, and re-layouts  93.1 us (14%)
  loops' own time  60.3 us (9%)
  other arithmetic  43.4 us (7%)
  between operations  13.7 us (2%)
  blocking collectives  10.8 us (2%)
    ppermute x16, starting transfers between devices, passed_along(): lax.ppermute(value, axis, [(source, source + steps) for source in range(i...  128 us
    reduce_scatter x2, waiting for transfers between devices, per_device(): lax.psum_scatter(rounded.astype(jnp.bfloat16), 'head', scatter_dimension=...  92.5 us
    dot_general x16, matrix products, one_head(): lax.dot_general(query_one, key_one, (((1,), (1,)), ((), ())), preferred_e...  88.3 us
    another operation x2, loops' own time, attend_local(): blended = lax.map(one_head, jnp.arange(local_heads, dtype=jnp.int32))  60 us
    all_gather x2, waiting for transfers between devices, per_device(): lax.all_gather(normed_part, 'head', axis=1, tiled=True)  43.6 us
    dot_general x16, matrix products, one_head(): jnp.dot(weights, value_one, preferred_element_type=jnp.float32)  25.5 us
    ppermute x16, waiting for transfers between devices, passed_along(): lax.ppermute(value, axis, [(source, source + steps) for source in range(i...  23.6 us
    dot_general x6, local copies, waits for them, and re-layouts, project_piece(): jnp.dot(piece_rows, weight, preferred_element_type=jnp.float32)  22.5 us
  transfers between devices with their start and end apart: 20, of which 20 were waited for; matrix products, arithmetic and copies ran while one was open for 4% of the time, Pallas kernels for 0%

commit v1 on v0

--- a/solution.py
+++ b/solution.py
@@ -10,6 +10,12 @@
 LAYER_COUNT = 2
 norm_epsilon = 1e-05
 rope_base = 10000.0
+
+
+def all_parts(x, axis, d):
+    terms = lax.all_gather(x, axis, axis=0, tiled=False)
+    result = jnp.concatenate(terms, axis=d)
+    return result
 
 
 def passed_along(value, axis, steps):
@@ -152,7 +158,7 @@
             jnp.zeros((rows_here, value_weight.shape[1]), jnp.float32),
         )
         query_raw, key_raw, value_raw = project_piece(
-            starting, lax.all_gather(normed_part, "head", axis=1, tiled=True), jnp.int32(0)
+            starting, all_parts(normed_part, "head", 1), jnp.int32(0)
         )
         queries = rotate_heads(query_raw, token_positions, local_query)
         keys_own = rotate_heads(key_raw, token_positions, local_kv).reshape(

time: 664 us -> 681 us (1.026)
  local copies, waits for them, and re-layouts: 93.1 us -> 113 us
    reshape x0 -> x4, local copies, waits for them, and re-layouts: none -> 9.58 us  [all_parts(): result = jnp.concatenate(terms, axis=d)]
where the time goes in v1:
time: 681 us; the launch traced here: 670 us
  waiting for transfers between devices  158 us (23%)
  matrix products  140 us (21%)
  starting transfers between devices  128 us (19%)
  local copies, waits for them, and re-layouts  113 us (17%)
  loops' own time  62.9 us (9%)
  other arithmetic  43.3 us (6%)
  between operations  13.7 us (2%)
  blocking collectives  10.8 us (2%)
    ppermute x16, starting transfers between devices, passed_along(): lax.ppermute(value, axis, [(source, source + steps) for source in range(i...  128 us
    reduce_scatter x2, waiting for transfers between devices, per_device(): lax.psum_scatter(rounded.astype(jnp.bfloat16), 'head', scatter_dimension=...  92.5 us
    dot_general x16, matrix products, one_head(): lax.dot_general(query_one, key_one, (((1,), (1,)), ((), ())), preferred_e...  88.1 us
    another operation x2, loops' own time, attend_local(): blended = lax.map(one_head, jnp.arange(local_heads, dtype=jnp.int32))  62.5 us
    all_gather x2, waiting for transfers between devices, all_parts(): terms = lax.all_gather(x, axis, axis=0, tiled=False)  42.1 us
    dot_general x16, matrix products, one_head(): jnp.dot(weights, value_one, preferred_element_type=jnp.float32)  25.5 us
    dot_general x6, local copies, waits for them, and re-layouts, project_piece(): jnp.dot(piece_rows, weight, preferred_element_type=jnp.float32)  24 us
    ppermute x16, waiting for transfers between devices, passed_along(): lax.ppermute(value, axis, [(source, source + steps) for source in range(i...  23.6 us
  transfers between devices with their start and end apart: 20, of which 20 were waited for; matrix products, arithmetic and copies ran while one was open for 4% of the time, Pallas kernels for 0%

profile of v1, /device:TPU:0, one launch (start us, length us, event | category | flops | bytes accessed | tf_op | source)
XLA Modules:
  0.0 670.0 jit_solution(1374829444870263825)
XLA Ops:
  26.5 6.6 copy.35
  35.2 17.1 %all-gather.5.cloned.1.call-done = bf16[1024,1024]{1,0:T(8,128)(2,1)} async-done(((bf16[512,1024]{1,0:T(8,128)(2,1)}), bf16[1024,1024]{1,0:T(8,128)(2,1)}) %all-gather.5.cloned.1.call-update) | async-done | bytes 2097168 | tf_op jit(solution)/shard_map/all_gather | solution.py:16
  67.5 83.0 %while.56 = (s32[]{:T(128)}, bf16[2,512,256]{2,1,0:T(8,128)(2,1)S(1)}, bf16[8,2,512,256]{3,2,1,0:T(8,128)(2,1)}, s32[]{:T(128)}, s32[]{:T(128)}, /*index=5*/s32[]{:T(128)}, s32[]{:T(128)}) while((s32[]{:T(128)}, bf16[2,512,256]{2,1,0:T(8,128)(2,1)S(1)}, bf16[8,2,512,256]{3,2,1,0:T(8,128)(2,1)}, s32[]{:T(128)}, s32[]{:T(128)}, ...), condition=%wide.region_3.4_spmd, body=%wide.region_2.3_spmd.sunk | while | flops 6 | bytes 4194471 | solution.py:113
  71.4 8.4 %collective-permute-start = (bf16[2,512,256]{2,1,0:T(8,128)(2,1)S(1)}, bf16[2,512,256]{2,1,0:T(8,128)(2,1)S(1)}, u32[]{:S(2)}, u32[]{:S(2)}) collective-permute-start(bf16[2,512,256]{2,1,0:T(8,128)(2,1)S(1)} %get-tuple-element.661), channel_id=1, source_target_pairs={{0,2},{2,4},{4,6},{6,8},{8,10},{10,12},{12,14},{14,16},{16,18},{18... | collective-permute-start | bytes 1572872 | tf_op jit(solution)/shard_map/while/body/eval_jaxpr/ppermute | solution.py:24
  82.2 9.0 %collective-permute-start = (bf16[2,512,256]{2,1,0:T(8,128)(2,1)S(1)}, bf16[2,512,256]{2,1,0:T(8,128)(2,1)S(1)}, u32[]{:S(2)}, u32[]{:S(2)}) collective-permute-start(bf16[2,512,256]{2,1,0:T(8,128)(2,1)S(1)} %get-tuple-element.661), channel_id=1, source_target_pairs={{0,2},{2,4},{4,6},{6,8},{8,10},{10,12},{12,14},{14,16},{16,18},{18... | collective-permute-start | bytes 1572872 | tf_op jit(solution)/shard_map/while/body/eval_jaxpr/ppermute | solution.py:24
  93.6 9.0 %collective-permute-start = (bf16[2,512,256]{2,1,0:T(8,128)(2,1)S(1)}, bf16[2,512,256]{2,1,0:T(8,128)(2,1)S(1)}, u32[]{:S(2)}, u32[]{:S(2)}) collective-permute-start(bf16[2,512,256]{2,1,0:T(8,128)(2,1)S(1)} %get-tuple-element.661), channel_id=1, source_target_pairs={{0,2},{2,4},{4,6},{6,8},{8,10},{10,12},{12,14},{14,16},{16,18},{18... | collective-permute-start | bytes 1572872 | tf_op jit(solution)/shard_map/while/body/eval_jaxpr/ppermute | solution.py:24
  105.0 9.0 %collective-permute-start = (bf16[2,512,256]{2,1,0:T(8,128)(2,1)S(1)}, bf16[2,512,256]{2,1,0:T(8,128)(2,1)S(1)}, u32[]{:S(2)}, u32[]{:S(2)}) collective-permute-start(bf16[2,512,256]{2,1,0:T(8,128)(2,1)S(1)} %get-tuple-element.661), channel_id=1, source_target_pairs={{0,2},{2,4},{4,6},{6,8},{8,10},{10,12},{12,14},{14,16},{16,18},{18... | collective-permute-start | bytes 1572872 | tf_op jit(solution)/shard_map/while/body/eval_jaxpr/ppermute | solution.py:24
  116.4 9.0 %collective-permute-start = (bf16[2,512,256]{2,1,0:T(8,128)(2,1)S(1)}, bf16[2,512,256]{2,1,0:T(8,128)(2,1)S(1)}, u32[]{:S(2)}, u32[]{:S(2)}) collective-permute-start(bf16[2,512,256]{2,1,0:T(8,128)(2,1)S(1)} %get-tuple-element.661), channel_id=1, source_target_pairs={{0,2},{2,4},{4,6},{6,8},{8,10},{10,12},{12,14},{14,16},{16,18},{18... | collective-permute-start | bytes 1572872 | tf_op jit(solution)/shard_map/while/body/eval_jaxpr/ppermute | solution.py:24
  127.7 9.0 %collective-permute-start = (bf16[2,512,256]{2,1,0:T(8,128)(2,1)S(1)}, bf16[2,512,256]{2,1,0:T(8,128)(2,1)S(1)}, u32[]{:S(2)}, u32[]{:S(2)}) collective-permute-start(bf16[2,512,256]{2,1,0:T(8,128)(2,1)S(1)} %get-tuple-element.661), channel_id=1, source_target_pairs={{0,2},{2,4},{4,6},{6,8},{8,10},{10,12},{12,14},{14,16},{16,18},{18... | collective-permute-start | bytes 1572872 | tf_op jit(solution)/shard_map/while/body/eval_jaxpr/ppermute | solution.py:24
  139.1 9.0 %collective-permute-start = (bf16[2,512,256]{2,1,0:T(8,128)(2,1)S(1)}, bf16[2,512,256]{2,1,0:T(8,128)(2,1)S(1)}, u32[]{:S(2)}, u32[]{:S(2)}) collective-permute-start(bf16[2,512,256]{2,1,0:T(8,128)(2,1)S(1)} %get-tuple-element.661), channel_id=1, source_target_pairs={{0,2},{2,4},{4,6},{6,8},{8,10},{10,12},{12,14},{14,16},{16,18},{18... | collective-permute-start | bytes 1572872 | tf_op jit(solution)/shard_map/while/body/eval_jaxpr/ppermute | solution.py:24
  174.1 112.1 %while.58 = (s32[]{:T(128)}, bf16[8,512,128]{1,2,0:T(8,128)(2,1)S(1)}, s32[8]{0:T(128)}, bf16[8,512,128]{1,2,0:T(8,128)(2,1)S(1)}, bf16[2,4608,128]{2,1,0:T(8,12...) while((s32[]{:T(128)}, ...), condition=%wide.region_8.9_spmd.clone, body=%wide.region_5.8_spmd.clone.sunk | while | flops 1238694912 | bytes 40932756 | solution.py:98
  292.2 46.2 %reduce-scatter.3.cloned.1.call-done = bf16[512,1024]{1,0:T(8,128)(2,1)} async-done(((bf16[512,2048]{1,0:T(8,128)(2,1)}), bf16[512,1024]{1,0:T(8,128)(2,1)}) %reduce-scatter.3.cloned.1.call-update) | async-done | bytes 1048592 | tf_op jit(solution)/shard_map/reduce_scatter | solution.py:175
  348.1 6.6 copy.43
  354.7 25.0 %all-gather.7.cloned.1.call-done = bf16[1024,1024]{1,0:T(8,128)(2,1)} async-done(((bf16[512,1024]{1,0:T(8,128)(2,1)}), bf16[1024,1024]{1,0:T(8,128)(2,1)}) %all-gather.7.cloned.1.call-update) | async-done | bytes 2097168 | tf_op jit(solution)/shard_map/all_gather | solution.py:16
  395.1 83.0 %while.57 = (s32[]{:T(128)}, bf16[2,512,256]{2,1,0:T(8,128)(2,1)S(1)}, bf16[8,2,512,256]{3,2,1,0:T(8,128)(2,1)}, s32[]{:T(128)}, s32[]{:T(128)}, /*index=5*/s32[]{:T(128)}, s32[]{:T(128)}) while((s32[]{:T(128)}, bf16[2,512,256]{2,1,0:T(8,128)(2,1)S(1)}, bf16[8,2,512,256]{3,2,1,0:T(8,128)(2,1)}, s32[]{:T(128)}, s32[]{:T(128)}, ...), condition=%wide.region_13.14_spmd, body=%wide.region_12.13_spmd.sunk | while | flops 6 | bytes 4194471 | solution.py:113
  399.0 8.4 %collective-permute-start.1 = (bf16[2,512,256]{2,1,0:T(8,128)(2,1)S(1)}, bf16[2,512,256]{2,1,0:T(8,128)(2,1)S(1)}, u32[]{:S(2)}, u32[]{:S(2)}) collective-permute-start(bf16[2,512,256]{2,1,0:T(8,128)(2,1)S(1)} %get-tuple-element.727), channel_id=1, source_target_pairs={{0,2},{2,4},{4,6},{6,8},{8,10},{10,12},{12,14},{14,16},{16,18},{18... | collective-permute-start | bytes 1572872 | tf_op jit(solution)/shard_map/while/body/eval_jaxpr/ppermute | solution.py:24
  409.8 9.0 %collective-permute-start.1 = (bf16[2,512,256]{2,1,0:T(8,128)(2,1)S(1)}, bf16[2,512,256]{2,1,0:T(8,128)(2,1)S(1)}, u32[]{:S(2)}, u32[]{:S(2)}) collective-permute-start(bf16[2,512,256]{2,1,0:T(8,128)(2,1)S(1)} %get-tuple-element.727), channel_id=1, source_target_pairs={{0,2},{2,4},{4,6},{6,8},{8,10},{10,12},{12,14},{14,16},{16,18},{18... | collective-permute-start | bytes 1572872 | tf_op jit(solution)/shard_map/while/body/eval_jaxpr/ppermute | solution.py:24
  421.2 9.0 %collective-permute-start.1 = (bf16[2,512,256]{2,1,0:T(8,128)(2,1)S(1)}, bf16[2,512,256]{2,1,0:T(8,128)(2,1)S(1)}, u32[]{:S(2)}, u32[]{:S(2)}) collective-permute-start(bf16[2,512,256]{2,1,0:T(8,128)(2,1)S(1)} %get-tuple-element.727), channel_id=1, source_target_pairs={{0,2},{2,4},{4,6},{6,8},{8,10},{10,12},{12,14},{14,16},{16,18},{18... | collective-permute-start | bytes 1572872 | tf_op jit(solution)/shard_map/while/body/eval_jaxpr/ppermute | solution.py:24
  432.6 9.0 %collective-permute-start.1 = (bf16[2,512,256]{2,1,0:T(8,128)(2,1)S(1)}, bf16[2,512,256]{2,1,0:T(8,128)(2,1)S(1)}, u32[]{:S(2)}, u32[]{:S(2)}) collective-permute-start(bf16[2,512,256]{2,1,0:T(8,128)(2,1)S(1)} %get-tuple-element.727), channel_id=1, source_target_pairs={{0,2},{2,4},{4,6},{6,8},{8,10},{10,12},{12,14},{14,16},{16,18},{18... | collective-permute-start | bytes 1572872 | tf_op jit(solution)/shard_map/while/body/eval_jaxpr/ppermute | solution.py:24
  444.0 9.0 %collective-permute-start.1 = (bf16[2,512,256]{2,1,0:T(8,128)(2,1)S(1)}, bf16[2,512,256]{2,1,0:T(8,128)(2,1)S(1)}, u32[]{:S(2)}, u32[]{:S(2)}) collective-permute-start(bf16[2,512,256]{2,1,0:T(8,128)(2,1)S(1)} %get-tuple-element.727), channel_id=1, source_target_pairs={{0,2},{2,4},{4,6},{6,8},{8,10},{10,12},{12,14},{14,16},{16,18},{18... | collective-permute-start | bytes 1572872 | tf_op jit(solution)/shard_map/while/body/eval_jaxpr/ppermute | solution.py:24
  455.4 9.0 %collective-permute-start.1 = (bf16[2,512,256]{2,1,0:T(8,128)(2,1)S(1)}, bf16[2,512,256]{2,1,0:T(8,128)(2,1)S(1)}, u32[]{:S(2)}, u32[]{:S(2)}) collective-permute-start(bf16[2,512,256]{2,1,0:T(8,128)(2,1)S(1)} %get-tuple-element.727), channel_id=1, source_target_pairs={{0,2},{2,4},{4,6},{6,8},{8,10},{10,12},{12,14},{14,16},{16,18},{18... | collective-permute-start | bytes 1572872 | tf_op jit(solution)/shard_map/while/body/eval_jaxpr/ppermute | solution.py:24
  466.7 9.0 %collective-permute-start.1 = (bf16[2,512,256]{2,1,0:T(8,128)(2,1)S(1)}, bf16[2,512,256]{2,1,0:T(8,128)(2,1)S(1)}, u32[]{:S(2)}, u32[]{:S(2)}) collective-permute-start(bf16[2,512,256]{2,1,0:T(8,128)(2,1)S(1)} %get-tuple-element.727), channel_id=1, source_target_pairs={{0,2},{2,4},{4,6},{6,8},{8,10},{10,12},{12,14},{14,16},{16,18},{18... | collective-permute-start | bytes 1572872 | tf_op jit(solution)/shard_map/while/body/eval_jaxpr/ppermute | solution.py:24
  500.6 107.6 %while.59 = (s32[]{:T(128)}, bf16[8,512,128]{1,2,0:T(8,128)(2,1)S(1)}, s32[8]{0:T(128)S(1)}, bf16[8,512,128]{1,2,0:T(8,128)(2,1)S(1)}, bf16[2,4608,128]{2,1,0:T(...) while((s32[]{:T(128)}, ...), condition=%wide.region_17.18_spmd.clone, body=%wide.region_14.17_spmd.clone.sunk | while | flops 1238694912 | bytes 40932756 | solution.py:98
  614.1 46.3 %reduce-scatter.5.cloned.1.call-done = bf16[512,1024]{1,0:T(8,128)(2,1)} async-done(((bf16[512,2048]{1,0:T(8,128)(2,1)}), bf16[512,1024]{1,0:T(8,128)(2,1)}) %reduce-scatter.5.cloned.1.call-update) | async-done | bytes 1048592 | tf_op jit(solution)/shard_map/reduce_scatter | solution.py:175
  (283 shorter events, 320.8 us)
Async XLA Ops:
  6.5 45.8 %all-gather.5.cloned.1.call-start = ((), (), s32[]{:S(2)}) async-start(), calls=%async_computation.4 | async-start | bytes 3145728 | tf_op jit(solution)/shard_map/all_gather | solution.py:16
  17.3 321.1 %reduce-scatter.3.cloned.1.call-start = ((), (), s32[]{:S(2)}) async-start(), calls=%async_computation.2 | async-start | bytes 3145728 | tf_op jit(solution)/shard_map/reduce_scatter | solution.py:175
  35.2 26.4 %copy-start.6 = (f32[512,64]{0,1:T(8,128)}, f32[512,64]{0,1:T(8,128)S(1)}, u32[]{:S(2)}) copy-start(f32[512,64]{0,1:T(8,128)S(1)} %get-tuple-element.494) | copy-start | bytes 393220
  67.5 3.1 collective-permute-start
  71.4 9.9 %collective-permute-start = (bf16[2,512,256]{2,1,0:T(8,128)(2,1)S(1)}, bf16[2,512,256]{2,1,0:T(8,128)(2,1)S(1)}, u32[]{:S(2)}, u32[]{:S(2)}) collective-permute-start(bf16[2,512,256]{2,1,0:T(8,128)(2,1)S(1)} %get-tuple-element.661), channel_id=1, source_target_pairs={{0,2},{2,4},{4,6},{6,8},{8,10},{10,12},{12,14},{14,16},{16,18},{18... | collective-permute-start | bytes 1572872 | tf_op jit(solution)/shard_map/while/body/eval_jaxpr/ppermute | solution.py:24
  82.2 10.5 %collective-permute-start = (bf16[2,512,256]{2,1,0:T(8,128)(2,1)S(1)}, bf16[2,512,256]{2,1,0:T(8,128)(2,1)S(1)}, u32[]{:S(2)}, u32[]{:S(2)}) collective-permute-start(bf16[2,512,256]{2,1,0:T(8,128)(2,1)S(1)} %get-tuple-element.661), channel_id=1, source_target_pairs={{0,2},{2,4},{4,6},{6,8},{8,10},{10,12},{12,14},{14,16},{16,18},{18... | collective-permute-start | bytes 1572872 | tf_op jit(solution)/shard_map/while/body/eval_jaxpr/ppermute | solution.py:24
  93.6 10.5 %collective-permute-start = (bf16[2,512,256]{2,1,0:T(8,128)(2,1)S(1)}, bf16[2,512,256]{2,1,0:T(8,128)(2,1)S(1)}, u32[]{:S(2)}, u32[]{:S(2)}) collective-permute-start(bf16[2,512,256]{2,1,0:T(8,128)(2,1)S(1)} %get-tuple-element.661), channel_id=1, source_target_pairs={{0,2},{2,4},{4,6},{6,8},{8,10},{10,12},{12,14},{14,16},{16,18},{18... | collective-permute-start | bytes 1572872 | tf_op jit(solution)/shard_map/while/body/eval_jaxpr/ppermute | solution.py:24
  105.0 10.5 %collective-permute-start = (bf16[2,512,256]{2,1,0:T(8,128)(2,1)S(1)}, bf16[2,512,256]{2,1,0:T(8,128)(2,1)S(1)}, u32[]{:S(2)}, u32[]{:S(2)}) collective-permute-start(bf16[2,512,256]{2,1,0:T(8,128)(2,1)S(1)} %get-tuple-element.661), channel_id=1, source_target_pairs={{0,2},{2,4},{4,6},{6,8},{8,10},{10,12},{12,14},{14,16},{16,18},{18... | collective-permute-start | bytes 1572872 | tf_op jit(solution)/shard_map/while/body/eval_jaxpr/ppermute | solution.py:24
  116.4 10.5 %collective-permute-start = (bf16[2,512,256]{2,1,0:T(8,128)(2,1)S(1)}, bf16[2,512,256]{2,1,0:T(8,128)(2,1)S(1)}, u32[]{:S(2)}, u32[]{:S(2)}) collective-permute-start(bf16[2,512,256]{2,1,0:T(8,128)(2,1)S(1)} %get-tuple-element.661), channel_id=1, source_target_pairs={{0,2},{2,4},{4,6},{6,8},{8,10},{10,12},{12,14},{14,16},{16,18},{18... | collective-permute-start | bytes 1572872 | tf_op jit(solution)/shard_map/while/body/eval_jaxpr/ppermute | solution.py:24
  127.7 10.5 %collective-permute-start = (bf16[2,512,256]{2,1,0:T(8,128)(2,1)S(1)}, bf16[2,512,256]{2,1,0:T(8,128)(2,1)S(1)}, u32[]{:S(2)}, u32[]{:S(2)}) collective-permute-start(bf16[2,512,256]{2,1,0:T(8,128)(2,1)S(1)} %get-tuple-element.661), channel_id=1, source_target_pairs={{0,2},{2,4},{4,6},{6,8},{8,10},{10,12},{12,14},{14,16},{16,18},{18... | collective-permute-start | bytes 1572872 | tf_op jit(solution)/shard_map/while/body/eval_jaxpr/ppermute | solution.py:24
  139.1 10.5 %collective-permute-start = (bf16[2,512,256]{2,1,0:T(8,128)(2,1)S(1)}, bf16[2,512,256]{2,1,0:T(8,128)(2,1)S(1)}, u32[]{:S(2)}, u32[]{:S(2)}) collective-permute-start(bf16[2,512,256]{2,1,0:T(8,128)(2,1)S(1)} %get-tuple-element.661), channel_id=1, source_target_pairs={{0,2},{2,4},{4,6},{6,8},{8,10},{10,12},{12,14},{14,16},{16,18},{18... | collective-permute-start | bytes 1572872 | tf_op jit(solution)/shard_map/while/body/eval_jaxpr/ppermute | solution.py:24
  292.1 46.3 %copy-start = (bf16[512,1024]{1,0:T(8,128)(2,1)S(1)}, bf16[512,1024]{1,0:T(8,128)(2,1)}, u32[]{:S(2)}) copy-start(bf16[512,1024]{1,0:T(8,128)(2,1)} %param.15) | copy-start | bytes 3145732
  292.1 87.6 %all-gather.7.cloned.1.call-start = ((), (), s32[]{:S(2)}) async-start(), calls=%async_computation.5 | async-start | bytes 3145728 | tf_op jit(solution)/shard_map/all_gather | solution.py:16
  338.4 6.7 copy-start.1
  346.5 314.0 %reduce-scatter.5.cloned.1.call-start = ((), (), s32[]{:S(2)}) async-start(), calls=%async_computation.3 | async-start | bytes 3145728 | tf_op jit(solution)/shard_map/reduce_scatter | solution.py:175
  395.1 3.1 collective-permute-start.1
  399.0 9.9 %collective-permute-start.1 = (bf16[2,512,256]{2,1,0:T(8,128)(2,1)S(1)}, bf16[2,512,256]{2,1,0:T(8,128)(2,1)S(1)}, u32[]{:S(2)}, u32[]{:S(2)}) collective-permute-start(bf16[2,512,256]{2,1,0:T(8,128)(2,1)S(1)} %get-tuple-element.727), channel_id=1, source_target_pairs={{0,2},{2,4},{4,6},{6,8},{8,10},{10,12},{12,14},{14,16},{16,18},{18... | collective-permute-start | bytes 1572872 | tf_op jit(solution)/shard_map/while/body/eval_jaxpr/ppermute | solution.py:24
  409.8 10.5 %collective-permute-start.1 = (bf16[2,512,256]{2,1,0:T(8,128)(2,1)S(1)}, bf16[2,512,256]{2,1,0:T(8,128)(2,1)S(1)}, u32[]{:S(2)}, u32[]{:S(2)}) collective-permute-start(bf16[2,512,256]{2,1,0:T(8,128)(2,1)S(1)} %get-tuple-element.727), channel_id=1, source_target_pairs={{0,2},{2,4},{4,6},{6,8},{8,10},{10,12},{12,14},{14,16},{16,18},{18... | collective-permute-start | bytes 1572872 | tf_op jit(solution)/shard_map/while/body/eval_jaxpr/ppermute | solution.py:24
  421.2 10.5 %collective-permute-start.1 = (bf16[2,512,256]{2,1,0:T(8,128)(2,1)S(1)}, bf16[2,512,256]{2,1,0:T(8,128)(2,1)S(1)}, u32[]{:S(2)}, u32[]{:S(2)}) collective-permute-start(bf16[2,512,256]{2,1,0:T(8,128)(2,1)S(1)} %get-tuple-element.727), channel_id=1, source_target_pairs={{0,2},{2,4},{4,6},{6,8},{8,10},{10,12},{12,14},{14,16},{16,18},{18... | collective-permute-start | bytes 1572872 | tf_op jit(solution)/shard_map/while/body/eval_jaxpr/ppermute | solution.py:24
  432.6 10.5 %collective-permute-start.1 = (bf16[2,512,256]{2,1,0:T(8,128)(2,1)S(1)}, bf16[2,512,256]{2,1,0:T(8,128)(2,1)S(1)}, u32[]{:S(2)}, u32[]{:S(2)}) collective-permute-start(bf16[2,512,256]{2,1,0:T(8,128)(2,1)S(1)} %get-tuple-element.727), channel_id=1, source_target_pairs={{0,2},{2,4},{4,6},{6,8},{8,10},{10,12},{12,14},{14,16},{16,18},{18... | collective-permute-start | bytes 1572872 | tf_op jit(solution)/shard_map/while/body/eval_jaxpr/ppermute | solution.py:24
  444.0 10.5 %collective-permute-start.1 = (bf16[2,512,256]{2,1,0:T(8,128)(2,1)S(1)}, bf16[2,512,256]{2,1,0:T(8,128)(2,1)S(1)}, u32[]{:S(2)}, u32[]{:S(2)}) collective-permute-start(bf16[2,512,256]{2,1,0:T(8,128)(2,1)S(1)} %get-tuple-element.727), channel_id=1, source_target_pairs={{0,2},{2,4},{4,6},{6,8},{8,10},{10,12},{12,14},{14,16},{16,18},{18... | collective-permute-start | bytes 1572872 | tf_op jit(solution)/shard_map/while/body/eval_jaxpr/ppermute | solution.py:24
  455.4 10.5 %collective-permute-start.1 = (bf16[2,512,256]{2,1,0:T(8,128)(2,1)S(1)}, bf16[2,512,256]{2,1,0:T(8,128)(2,1)S(1)}, u32[]{:S(2)}, u32[]{:S(2)}) collective-permute-start(bf16[2,512,256]{2,1,0:T(8,128)(2,1)S(1)} %get-tuple-element.727), channel_id=1, source_target_pairs={{0,2},{2,4},{4,6},{6,8},{8,10},{10,12},{12,14},{14,16},{16,18},{18... | collective-permute-start | bytes 1572872 | tf_op jit(solution)/shard_map/while/body/eval_jaxpr/ppermute | solution.py:24
  466.7 10.5 %collective-permute-start.1 = (bf16[2,512,256]{2,1,0:T(8,128)(2,1)S(1)}, bf16[2,512,256]{2,1,0:T(8,128)(2,1)S(1)}, u32[]{:S(2)}, u32[]{:S(2)}) collective-permute-start(bf16[2,512,256]{2,1,0:T(8,128)(2,1)S(1)} %get-tuple-element.727), channel_id=1, source_target_pairs={{0,2},{2,4},{4,6},{6,8},{8,10},{10,12},{12,14},{14,16},{16,18},{18... | collective-permute-start | bytes 1572872 | tf_op jit(solution)/shard_map/while/body/eval_jaxpr/ppermute | solution.py:24
  614.1 46.3 %copy-start.2 = (bf16[512,1024]{1,0:T(8,128)(2,1)S(1)}, bf16[512,1024]{1,0:T(8,128)(2,1)}, u32[]{:S(2)}) copy-start(bf16[512,1024]{1,0:T(8,128)(2,1)} %reduce-scatter.3.cloned.1.call-done) | copy-start | bytes 3145732
  (27 other events, 57.1 us)
Sparse Core Ops, SparseCore 0:
  17.4 34.8 all-gather.4
  292.2 46.1 reduce-scatter.2
  346.6 33.0 all-gather.6
  614.3 46.1 reduce-scatter.4
